TPU v7x, 32 devices: a whole 2x2x4 slice. The times are simulated.
32 devices in a mesh: gx: 8 (over z, x), gy: 4 (over y, core).
Axes of the slice: x: 2, y: 2, z: 4, core: 2. Of those that a mesh axis runs over, the one named last changes fastest.
Arguments:
- level_set: float32 [256, 128, 128], P('gx', 'gy'), may hold values from -6 to 6
- sensitivity: float32 [256, 128, 128], P('gx', 'gy'), may hold values from -6 to 6
- smooth_taps: float32 [25], replicated, may hold values from 0.1 to 0.3
- slope_taps: float32 [25], replicated, as said below
- band: int32 [16, 8, 4], P('gx', 'gy'), may hold values from 0 to 1
- time_step: float32 [1], replicated, may hold values from 0.05 to 0.15
Outputs:
- updated: float32 [256, 128, 128], P('gx', 'gy')
Inputs may be any that keep to these rules, and one draw needn't show every extreme that they name: slope_taps[24 - k] = -slope_taps[k]; the middle tap is zero.
All inputs are finite; a program needn't handle non-finite values.
Results may differ from a plain program's by a relative error of at most 0.00002.
Values sent between devices are 32-bit elements; how exact they have to be, the bound alone decides.
A program may use at most 64 MiB of HBM per device.

v0:
```python
import jax
import jax.numpy as jnp
from jax import lax
from jax.sharding import PartitionSpec as P

UPDATES = 2


opening_depth = ((0, 0), (1, 0), (1, 1))
opening_cross = ((0, 0), (1, 0), (1, 1), (2, 0))
opening_along = ((0, 0), (2, 0), (1, 1), (3, 0))
later_depth = ((0, 0), (0, 1))
later_cross = ((0, 0), (0, 1), (1, 0))
later_along = ((1, 0), (0, 1), (2, 0))


def with_halo(block, sides, width):
    for axis, dim in sides:
        count = lax.axis_size(axis)
        forward = [(i, i + 1) for i in range(count - 1)]
        backward = [(target, source) for source, target in forward]
        low = lax.ppermute(
            lax.slice_in_dim(block, block.shape[dim] - width, None, axis=dim), axis, forward
        )
        high = lax.ppermute(lax.slice_in_dim(block, 0, width, axis=dim), axis, backward)
        block = jnp.concatenate([low, block, high], axis=dim)
    return block


def pad_margin(stack, axis):
    widths = [(0, 0)] * stack.ndim
    widths[axis] = (12, 12)
    return jnp.pad(stack, widths)


def taps_sum(padded, taps, axis, length):
    summed = taps[0] * lax.slice_in_dim(padded, 0, length, axis=axis)
    for offset in range(1, 25):
        summed = summed + taps[offset] * lax.slice_in_dim(
            padded, offset, offset + length, axis=axis
        )
    return summed


def apply_plan(padded, plan, tap_sets, axis, length):
    results = [
        taps_sum(padded[source], tap_sets[filter_kind], axis - 1, length)
        for source, filter_kind in plan
    ]
    return jnp.stack(results)


def inside_domain(count, rows, position, devices):
    first = position * rows - 1
    places = first + jnp.arange(count, dtype=jnp.int32)
    total = rows * devices
    return ((places >= 0) & (places < total)).astype(jnp.float32)


def per_device(level_set, sensitivity, smooth_taps, slope_taps, band, time_step):
    rows_x, rows_y, depth = level_set.shape
    tap_sets = (smooth_taps, slope_taps)
    blocks_x, blocks_y, blocks_z = band.shape
    mask = jnp.broadcast_to(
        band.astype(jnp.float32)[:, None, :, None, :, None],
        (blocks_x, rows_x // blocks_x, blocks_y, rows_y // blocks_y, blocks_z, depth // blocks_z),
    ).reshape(rows_x, rows_y, depth)
    step_size = time_step[0]
    phi = level_set
    speed = jnp.zeros_like(level_set)
    for update_index in range(UPDATES):
        if update_index == 0:
            fields = jnp.stack([sensitivity, phi])
            plans = (opening_depth, opening_cross, opening_along)
        else:
            fields = phi[None]
            plans = (later_depth, later_cross, later_along)
        widened = with_halo(fields, (("gx", 1), ("gy", 2)), 13)
        depth_out = apply_plan(pad_margin(widened, 3), plans[0], tap_sets, 3, depth)
        keep_x = inside_domain(rows_x + 2, rows_x, lax.axis_index("gx"), lax.axis_size("gx"))
        cross_out = apply_plan(depth_out, plans[1], tap_sets, 1, rows_x + 2)
        cross_out = cross_out * keep_x[None, :, None, None]
        keep_y = inside_domain(rows_y + 2, rows_y, lax.axis_index("gy"), lax.axis_size("gy"))
        along_out = apply_plan(cross_out, plans[2], tap_sets, 2, rows_y + 2)
        along_out = along_out * keep_y[None, None, :, None]
        if update_index == 0:
            velocity_block = along_out[0]
            gradient = along_out[1:]
        else:
            gradient = along_out
        magnitude_block = jnp.sqrt(
            gradient[0] * gradient[0] + gradient[1] * gradient[1] + gradient[2] * gradient[2] + 1.0
        )
        normal_x = gradient[0] / magnitude_block
        normal_y = gradient[1] / magnitude_block
        normal_z = gradient[2, 1:-1, 1:-1] / magnitude_block[1:-1, 1:-1]
        magnitude = magnitude_block[1:-1, 1:-1]
        depth_normal = jnp.pad(normal_z, ((0, 0), (0, 0), (1, 1)))
        curvature = (
            0.5 * (normal_x[2:, 1:-1] - normal_x[:-2, 1:-1])
            + 0.5 * (normal_y[1:-1, 2:] - normal_y[1:-1, :-2])
            + 0.5 * (depth_normal[:, :, 2:] - depth_normal[:, :, :-2])
        )
        if update_index == 0:
            depth_velocity = jnp.pad(velocity_block[1:-1, 1:-1], ((0, 0), (0, 0), (1, 1)))
            speed = (
                velocity_block[1:-1, 1:-1]
                + velocity_block[2:, 1:-1]
                + velocity_block[:-2, 1:-1]
                + velocity_block[1:-1, 2:]
                + velocity_block[1:-1, :-2]
                + depth_velocity[:, :, 2:]
                + depth_velocity[:, :, :-2]
            ) / 7.0
        phi = phi - mask * step_size * magnitude * (speed - 0.5 * curvature)
    return phi


def solution(mesh):
    return jax.shard_map(
        per_device,
        mesh=mesh,
        in_specs=(P("gx", "gy", None), P("gx", "gy", None), P(), P(), P("gx", "gy", None), P()),
        out_specs=P("gx", "gy", None),
        check_vma=False,
    )
```

profile of v0, /device:TPU:19, one launch (start us, length us, event | category | flops | bytes accessed | tf_op | source)
XLA Modules:
  0.0 521.5 jit_solution(2039735928300474859)
XLA Ops:
  0.0 2.1 pad_maximum_fusion.6
  2.1 3.2 collective-permute-start
  5.3 2.1 collective-permute-start.1
  8.1 15.8 %collective-permute-done = f32[2,13,32,128]{3,0,2,1:T(2,128)S(1)} collective-permute-done((f32[2,13,32,128]{3,0,2,1:T(2,128)S(1)}, f32[2,13,32,128]{3,0,2,1:T(2,128)S(1)}, u32[]{:S(2)}, u32[]{:S(2)}) %collective-permute-start) | collective-permute-done | bytes 426016 | tf_op jit(solution)/shard_map/ppermute | solution.py:22
  23.9 0.8 copy-done.6
  24.6 5.2 pad_maximum_fusion.4
  29.8 4.6 collective-permute-start.2
  34.4 2.1 collective-permute-start.3
  37.1 1.7 mul.2308
  40.1 0.7 fusion.313
  40.9 0.7 fusion.315
  41.6 1.9 collective-permute-done.2
  43.5 4.4 collective-permute-done.3
  47.9 32.4 %select_maximum_fusion = f32[2,58,58,152]{3,0,2,1:T(2,128)S(1)} fusion(f32[2,58,13,128]{3,0,2,1:T(2,128)} %collective-permute-done.3, f32[2,58,13,128]{3,0,2,1:T(2,128)} %collective-permute-done.2, f32[2,13,32,128]{3,0,2,1:T(2,128)} %copy-done.7, f32[2,13,32,128]{3,0,2,1:T(2,128)} %copy-done.6, f32[1,32,32,128]{3,0,2,1:T(1,128)S(1)} %bitcast.169, ...), kind=kLoop, calls=%fused_computation.1 | loop fusion | flops 14317184 | bytes 7535360 | tf_op jit(solution)/shard_map/concatenate | solution.py:26
  80.2 4.7 fusion.310
  85.5 27.8 %multiply_add_fusion.3 = f32[58,58,128]{2,1,0:T(8,128)S(1)} fusion(f32[58,58,152]{2,1,0:T(8,128)S(1)} %bitcast.161, f32[]{:T(128)} %bitcast.28, f32[]{:T(128)} %bitcast.27, f32[]{:T(128)} %bitcast.26, f32[]{:T(128)} %bitcast.25, f32[]{:T(128)} %bitcast.24, f32[]{:T(128)} %bitcast.23, f32[]{:T(128)} %bitcast.22, f32[]{:T(128)} %bitcast.21, f32[]{:T(128)} %bitcast.20, ...), kind=kLoop, calls=%fused_computation.72 | loop fusion | flops 21099008 | bytes 44781668 | tf_op jit(solution)/shard_map/add | solution.py:39
  113.3 20.0 %add_bitcast_fusion.3 = f32[1,34,58,128]{3,2,1,0:T(8,128)} fusion(f32[58,58,128]{2,1,0:T(8,128)S(1)} %multiply_add_fusion.3, f32[]{:T(128)} %bitcast.28, f32[]{:T(128)} %bitcast.27, f32[]{:T(128)} %bitcast.26, f32[]{:T(128)} %bitcast.25, f32[]{:T(128)} %bitcast.24, f32[]{:T(128)} %bitcast.23, f32[]{:T(128)} %bitcast.22, f32[]{:T(128)} %bitcast.21, ...), kind=kLoop, calls=%fused_computation.239 | loop fusion | flops 12368384 | bytes 26251364 | tf_op jit(solution)/shard_map/stack | solution.py:50
  133.2 19.7 %add_bitcast_fusion.2 = f32[1,34,58,128]{3,2,1,0:T(8,128)} fusion(f32[58,58,128]{2,1,0:T(8,128)S(1)} %multiply_add_fusion.3, f32[]{:T(128)} %bitcast.55, f32[]{:T(128)} %bitcast.54, f32[]{:T(128)} %bitcast.53, f32[]{:T(128)} %bitcast.52, f32[]{:T(128)} %bitcast.51, f32[]{:T(128)} %bitcast.50, f32[]{:T(128)} %bitcast.49, f32[]{:T(128)} %bitcast.48, ...), kind=kLoop, calls=%fused_computation.238 | loop fusion | flops 12368384 | bytes 26251364 | tf_op jit(solution)/shard_map/stack | solution.py:50
  153.0 28.0 %multiply_add_fusion.2 = f32[58,58,128]{2,1,0:T(8,128)S(1)} fusion(f32[58,58,152]{2,1,0:T(8,128)S(1)} %bitcast.162, f32[]{:T(128)} %bitcast.55, f32[]{:T(128)} %bitcast.54, f32[]{:T(128)} %bitcast.53, f32[]{:T(128)} %bitcast.52, f32[]{:T(128)} %bitcast.51, f32[]{:T(128)} %bitcast.50, f32[]{:T(128)} %bitcast.49, f32[]{:T(128)} %bitcast.48, f32[]{:T(128)} %bitcast.47, ...), kind=kLoop, calls=%fused_computation.71 | loop fusion | flops 21099008 | bytes 44781668 | tf_op jit(solution)/shard_map/add | solution.py:39
  181.5 27.8 %fusion.2 = f32[58,58,128]{2,1,0:T(8,128)S(1)} fusion(f32[58,58,152]{2,1,0:T(8,128)S(1)} %bitcast.163, f32[]{:T(128)} %bitcast.28, f32[]{:T(128)} %bitcast.27, f32[]{:T(128)} %bitcast.26, f32[]{:T(128)} %bitcast.25, f32[]{:T(128)} %bitcast.24, f32[]{:T(128)} %bitcast.23, f32[]{:T(128)} %bitcast.22, f32[]{:T(128)} %bitcast.21, f32[]{:T(128)} %bitcast.20, ...), kind=kLoop, calls=%fused_computation.21 | loop fusion | flops 21099008 | bytes 44781668 | tf_op jit(solution)/shard_map/add | solution.py:39
  209.3 19.2 %fusion.77 = f32[1,34,58,128]{3,2,1,0:T(8,128)S(1)} fusion(f32[58,58,128]{2,1,0:T(8,128)S(1)} %fusion.2, f32[]{:T(128)} %bitcast.28, f32[]{:T(128)} %bitcast.27, f32[]{:T(128)} %bitcast.26, f32[]{:T(128)} %bitcast.25, f32[]{:T(128)} %bitcast.24, f32[]{:T(128)} %bitcast.23, f32[]{:T(128)} %bitcast.22, f32[]{:T(128)} %bitcast.21, f32[]{:T(128)} %bitcast.20, ...), kind=kLoop, calls=%fused_computation.188 | loop fusion | flops 12368384 | bytes 26251364 | tf_op jit(solution)/shard_map/stack | solution.py:50
  228.5 19.3 %fusion.52 = f32[1,34,58,128]{3,2,1,0:T(8,128)S(1)} fusion(f32[58,58,128]{2,1,0:T(8,128)S(1)} %multiply_add_fusion.2, f32[]{:T(128)} %bitcast.28, f32[]{:T(128)} %bitcast.27, f32[]{:T(128)} %bitcast.26, f32[]{:T(128)} %bitcast.25, f32[]{:T(128)} %bitcast.24, f32[]{:T(128)} %bitcast.23, f32[]{:T(128)} %bitcast.22, f32[]{:T(128)} %bitcast.21, f32[]{:T(128)} %bitcast.20, ...), kind=kLoop, calls=%fused_computation.138 | loop fusion | flops 12368384 | bytes 26251364 | tf_op jit(solution)/shard_map/stack | solution.py:50
  247.8 0.9 maximum_multiply_fusion
  249.4 17.6 %fusion.210 = f32[1,34,34,128]{3,2,1,0:T(8,128)S(1)} fusion(f32[34,58,128]{2,1,0:T(8,128)S(1)} %get-tuple-element.15, f32[]{:T(128)} %bitcast.55, f32[]{:T(128)} %bitcast.54, f32[]{:T(128)} %bitcast.53, f32[]{:T(128)} %bitcast.52, f32[]{:T(128)} %bitcast.51, f32[]{:T(128)} %bitcast.50, f32[]{:T(128)} %bitcast.49, f32[]{:T(128)} %bitcast.48, f32[]{:T(128)} %bitcast.47, ...), kind=kLoop, calls=%fused_computation.462 | loop fusion | flops 7250432 | bytes 15388772 | tf_op jit(solution)/shard_map/stack | solution.py:50
  267.0 18.0 %fusion.235 = f32[1,34,34,128]{3,2,1,0:T(8,128)S(1)} fusion(f32[34,58,128]{2,1,0:T(8,128)S(1)} %get-tuple-element.16, f32[]{:T(128)} %bitcast.28, f32[]{:T(128)} %bitcast.27, f32[]{:T(128)} %bitcast.26, f32[]{:T(128)} %bitcast.25, f32[]{:T(128)} %bitcast.24, f32[]{:T(128)} %bitcast.23, f32[]{:T(128)} %bitcast.22, f32[]{:T(128)} %bitcast.21, f32[]{:T(128)} %bitcast.20, ...), kind=kLoop, calls=%fused_computation.512 | loop fusion | flops 7250432 | bytes 15388772 | tf_op jit(solution)/shard_map/stack | solution.py:50
  285.0 17.8 %fusion.260 = f32[1,34,34,128]{3,2,1,0:T(8,128)S(1)} fusion(f32[34,58,128]{2,1,0:T(8,128)S(1)} %get-tuple-element.13, f32[]{:T(128)} %bitcast.28, f32[]{:T(128)} %bitcast.27, f32[]{:T(128)} %bitcast.26, f32[]{:T(128)} %bitcast.25, f32[]{:T(128)} %bitcast.24, f32[]{:T(128)} %bitcast.23, f32[]{:T(128)} %bitcast.22, f32[]{:T(128)} %bitcast.21, f32[]{:T(128)} %bitcast.20, ...), kind=kLoop, calls=%fused_computation.562 | loop fusion | flops 7250432 | bytes 15388772 | tf_op jit(solution)/shard_map/stack | solution.py:50
  302.8 17.8 %fusion.185 = f32[1,34,34,128]{3,2,1,0:T(8,128)S(1)} fusion(f32[34,58,128]{2,1,0:T(8,128)S(1)} %get-tuple-element.14, f32[]{:T(128)} %bitcast.28, f32[]{:T(128)} %bitcast.27, f32[]{:T(128)} %bitcast.26, f32[]{:T(128)} %bitcast.25, f32[]{:T(128)} %bitcast.24, f32[]{:T(128)} %bitcast.23, f32[]{:T(128)} %bitcast.22, f32[]{:T(128)} %bitcast.21, f32[]{:T(128)} %bitcast.20, ...), kind=kLoop, calls=%fused_computation.412 | loop fusion | flops 7250432 | bytes 15388772 | tf_op jit(solution)/shard_map/stack | solution.py:50
  321.6 0.9 copy-done.1
  322.5 1.5 fusion.296
  324.1 3.3 collective-permute-start.4
  327.4 1.9 collective-permute-start.5
  329.4 1.5 collective-permute-done.4
  330.9 4.0 collective-permute-done.5
  335.1 3.2 collective-permute-start.6
  338.2 1.9 collective-permute-start.7
  340.2 3.6 collective-permute-done.6
  343.8 4.4 collective-permute-done.7
  348.2 3.3 fusion
  351.5 27.8 %multiply_add_fusion.1 = f32[58,58,128]{2,1,0:T(8,128)S(1)} fusion(f32[58,58,152]{2,1,0:T(8,128)S(1)} %fusion, f32[]{:T(128)} %bitcast.28, f32[]{:T(128)} %bitcast.27, f32[]{:T(128)} %bitcast.26, f32[]{:T(128)} %bitcast.25, f32[]{:T(128)} %bitcast.24, f32[]{:T(128)} %bitcast.23, f32[]{:T(128)} %bitcast.22, f32[]{:T(128)} %bitcast.21, f32[]{:T(128)} %bitcast.20, ...), kind=kLoop, calls=%fused_computation.70 | loop fusion | flops 21099008 | bytes 44781668 | tf_op jit(solution)/shard_map/add | solution.py:39
  379.3 19.0 %add_bitcast_fusion = f32[1,34,58,128]{3,2,1,0:T(8,128)S(1)} fusion(f32[58,58,128]{2,1,0:T(8,128)S(1)} %multiply_add_fusion.1, f32[]{:T(128)} %bitcast.55, f32[]{:T(128)} %bitcast.54, f32[]{:T(128)} %bitcast.53, f32[]{:T(128)} %bitcast.52, f32[]{:T(128)} %bitcast.51, f32[]{:T(128)} %bitcast.50, f32[]{:T(128)} %bitcast.49, f32[]{:T(128)} %bitcast.48, ...), kind=kLoop, calls=%fused_computation.236 | loop fusion | flops 12368384 | bytes 26251364 | tf_op jit(solution)/shard_map/stack | solution.py:50
  398.3 19.2 %add_bitcast_fusion.1 = f32[1,34,58,128]{3,2,1,0:T(8,128)S(1)} fusion(f32[58,58,128]{2,1,0:T(8,128)S(1)} %multiply_add_fusion.1, f32[]{:T(128)} %bitcast.28, f32[]{:T(128)} %bitcast.27, f32[]{:T(128)} %bitcast.26, f32[]{:T(128)} %bitcast.25, f32[]{:T(128)} %bitcast.24, f32[]{:T(128)} %bitcast.23, f32[]{:T(128)} %bitcast.22, f32[]{:T(128)} %bitcast.21, ...), kind=kLoop, calls=%fused_computation.237 | loop fusion | flops 12368384 | bytes 26251364 | tf_op jit(solution)/shard_map/stack | solution.py:50
  417.5 27.6 %multiply_add_fusion = f32[58,58,128]{2,1,0:T(8,128)S(1)} fusion(f32[58,58,152]{2,1,0:T(8,128)S(1)} %fusion, f32[]{:T(128)} %bitcast.55, f32[]{:T(128)} %bitcast.54, f32[]{:T(128)} %bitcast.53, f32[]{:T(128)} %bitcast.52, f32[]{:T(128)} %bitcast.51, f32[]{:T(128)} %bitcast.50, f32[]{:T(128)} %bitcast.49, f32[]{:T(128)} %bitcast.48, f32[]{:T(128)} %bitcast.47, ...), kind=kLoop, calls=%fused_computation.69 | loop fusion | flops 21099008 | bytes 44781668 | tf_op jit(solution)/shard_map/add | solution.py:39
  445.1 19.3 %fusion.27 = f32[1,34,58,128]{3,2,1,0:T(8,128)S(1)} fusion(f32[58,58,128]{2,1,0:T(8,128)S(1)} %multiply_add_fusion, f32[]{:T(128)} %bitcast.28, f32[]{:T(128)} %bitcast.27, f32[]{:T(128)} %bitcast.26, f32[]{:T(128)} %bitcast.25, f32[]{:T(128)} %bitcast.24, f32[]{:T(128)} %bitcast.23, f32[]{:T(128)} %bitcast.22, f32[]{:T(128)} %bitcast.21, f32[]{:T(128)} %bitcast.20, ...), kind=kLoop, calls=%fused_computation.84 | loop fusion | flops 12368384 | bytes 26251364 | tf_op jit(solution)/shard_map/stack | solution.py:50
  465.0 17.6 %fusion.131 = f32[1,34,34,128]{3,2,1,0:T(8,128)S(1)} fusion(f32[34,58,128]{2,1,0:T(8,128)S(1)} %get-tuple-element.19, f32[]{:T(128)} %bitcast.55, f32[]{:T(128)} %bitcast.54, f32[]{:T(128)} %bitcast.53, f32[]{:T(128)} %bitcast.52, f32[]{:T(128)} %bitcast.51, f32[]{:T(128)} %bitcast.50, f32[]{:T(128)} %bitcast.49, f32[]{:T(128)} %bitcast.48, f32[]{:T(128)} %bitcast.47, ...), kind=kLoop, calls=%fused_computation.304 | loop fusion | flops 7250432 | bytes 15388772 | tf_op jit(solution)/shard_map/stack | solution.py:50
  482.6 17.8 %fusion.156 = f32[1,34,34,128]{3,2,1,0:T(8,128)S(1)} fusion(f32[34,58,128]{2,1,0:T(8,128)S(1)} %get-tuple-element.17, f32[]{:T(128)} %bitcast.28, f32[]{:T(128)} %bitcast.27, f32[]{:T(128)} %bitcast.26, f32[]{:T(128)} %bitcast.25, f32[]{:T(128)} %bitcast.24, f32[]{:T(128)} %bitcast.23, f32[]{:T(128)} %bitcast.22, f32[]{:T(128)} %bitcast.21, f32[]{:T(128)} %bitcast.20, ...), kind=kLoop, calls=%fused_computation.354 | loop fusion | flops 7250432 | bytes 15388772 | tf_op jit(solution)/shard_map/stack | solution.py:50
  500.5 17.8 %fusion.106 = f32[1,34,34,128]{3,2,1,0:T(8,128)S(1)} fusion(f32[34,58,128]{2,1,0:T(8,128)S(1)} %get-tuple-element.18, f32[]{:T(128)} %bitcast.28, f32[]{:T(128)} %bitcast.27, f32[]{:T(128)} %bitcast.26, f32[]{:T(128)} %bitcast.25, f32[]{:T(128)} %bitcast.24, f32[]{:T(128)} %bitcast.23, f32[]{:T(128)} %bitcast.22, f32[]{:T(128)} %bitcast.21, f32[]{:T(128)} %bitcast.20, ...), kind=kLoop, calls=%fused_computation.254 | loop fusion | flops 7250432 | bytes 15388772 | tf_op jit(solution)/shard_map/stack | solution.py:50
  519.2 0.9 copy-done.5
  520.0 1.3 fusion.302
  (44 shorter events, 6.2 us)
Async XLA Ops:
  0.0 24.6 %copy-start.2 = (f32[32,32,128]{2,1,0:T(8,128)S(1)}, f32[32,32,128]{2,1,0:T(8,128)}, u32[]{:S(2)}) copy-start(f32[32,32,128]{2,1,0:T(8,128)} %param.7) | copy-start | bytes 1572868
  0.0 24.6 %copy-start = (f32[32,32,128]{2,1,0:T(8,128)S(1)}, f32[32,32,128]{2,1,0:T(8,128)}, u32[]{:S(2)}) copy-start(f32[32,32,128]{2,1,0:T(8,128)} %param.6) | copy-start | bytes 1572868
  2.1 21.7 %collective-permute-start = (f32[2,13,32,128]{3,0,2,1:T(2,128)S(1)}, f32[2,13,32,128]{3,0,2,1:T(2,128)S(1)}, u32[]{:S(2)}, u32[]{:S(2)}) collective-permute-start(f32[2,13,32,128]{3,0,2,1:T(2,128)S(1)} %get-tuple-element.22), channel_id=1, source_target_pairs={{0,4},{4,8},{8,12},{12,16},{16,20},{20,24},{24,28},{1,5},{5,9},{9,... | collective-permute-start | bytes 1277960 | tf_op jit(solution)/shard_map/ppermute | solution.py:22
  5.3 18.5 %collective-permute-start.1 = (f32[2,13,32,128]{3,0,2,1:T(2,128)S(1)}, f32[2,13,32,128]{3,0,2,1:T(2,128)S(1)}, u32[]{:S(2)}, u32[]{:S(2)}) collective-permute-start(f32[2,13,32,128]{3,0,2,1:T(2,128)S(1)} %get-tuple-element.23), channel_id=1, source_target_pairs={{4,0},{8,4},{12,8},{16,12},{20,16},{24,20},{28,24},{5,1},{9,5},{13... | collective-permute-start | bytes 1277960 | tf_op jit(solution)/shard_map/ppermute | solution.py:25
  8.1 28.4 %copy-start.10 = (s32[2,2,4]{2,1,0:T(2,128)S(1)}, s32[2,2,4]{2,1,0:T(2,128)}, u32[]{:S(2)}) copy-start(s32[2,2,4]{2,1,0:T(2,128)} %param.10) | copy-start | bytes 196
  23.9 0.8 copy-start.6
  24.6 5.2 copy-start.7
  29.8 13.6 %collective-permute-start.2 = (f32[2,58,13,128]{3,0,2,1:T(2,128)}, f32[2,58,13,128]{3,0,2,1:T(2,128)}, u32[]{:S(2)}, u32[]{:S(2)}) collective-permute-start(f32[2,58,13,128]{3,0,2,1:T(2,128)} %get-tuple-element.20), channel_id=1, source_target_pairs={{0,1},{1,2},{2,3},{4,5},{5,6},{6,7},{8,9},{9,10},{10,11},{12,13},{... | collective-permute-start | bytes 2316296 | tf_op jit(solution)/shard_map/ppermute | solution.py:22
  34.4 13.5 %collective-permute-start.3 = (f32[2,58,13,128]{3,0,2,1:T(2,128)}, f32[2,58,13,128]{3,0,2,1:T(2,128)}, u32[]{:S(2)}, u32[]{:S(2)}) collective-permute-start(f32[2,58,13,128]{3,0,2,1:T(2,128)} %get-tuple-element.21), channel_id=1, source_target_pairs={{1,0},{2,1},{3,2},{5,4},{6,5},{7,6},{9,8},{10,9},{11,10},{13,12},{... | collective-permute-start | bytes 2316296 | tf_op jit(solution)/shard_map/ppermute | solution.py:25
  37.1 1.7 copy-start.8
  37.1 2.4 copy-start.9
  228.5 19.4 %copy-start.3 = (f32[1,34,58,128]{3,2,1,0:T(8,128)S(1)}, f32[1,34,58,128]{3,2,1,0:T(8,128)}, u32[]{:S(2)}) copy-start(f32[1,34,58,128]{3,2,1,0:T(8,128)} %add_bitcast_fusion.3) | copy-start | bytes 3028996
  228.5 19.4 %copy-start.4 = (f32[1,34,58,128]{3,2,1,0:T(8,128)S(1)}, f32[1,34,58,128]{3,2,1,0:T(8,128)}, u32[]{:S(2)}) copy-start(f32[1,34,58,128]{3,2,1,0:T(8,128)} %add_bitcast_fusion.2) | copy-start | bytes 3028996
  321.5 1.0 copy-start.1
  324.1 6.8 %collective-permute-start.4 = (f32[1,13,32,128]{3,2,1,0:T(8,128)S(1)}, f32[1,13,32,128]{3,2,1,0:T(8,128)S(1)}, u32[]{:S(2)}, u32[]{:S(2)}) collective-permute-start(f32[1,13,32,128]{3,2,1,0:T(8,128)S(1)} %get-tuple-element.26), channel_id=1, source_target_pairs={{0,4},{4,8},{8,12},{12,16},{16,20},{20,24},{24,28},{1,5},{5,9},{9,... | collective-permute-start | bytes 638984 | tf_op jit(solution)/shard_map/ppermute | solution.py:22
  327.4 7.5 %collective-permute-start.5 = (f32[1,13,32,128]{3,2,1,0:T(8,128)S(1)}, f32[1,13,32,128]{3,2,1,0:T(8,128)S(1)}, u32[]{:S(2)}, u32[]{:S(2)}) collective-permute-start(f32[1,13,32,128]{3,2,1,0:T(8,128)S(1)} %get-tuple-element.27), channel_id=1, source_target_pairs={{4,0},{8,4},{12,8},{16,12},{20,16},{24,20},{28,24},{5,1},{9,5},{13... | collective-permute-start | bytes 638984 | tf_op jit(solution)/shard_map/ppermute | solution.py:25
  335.1 8.8 %collective-permute-start.6 = (f32[1,58,13,128]{3,2,1,0:T(8,128)S(1)}, f32[1,58,13,128]{3,2,1,0:T(8,128)S(1)}, u32[]{:S(2)}, u32[]{:S(2)}) collective-permute-start(f32[1,58,13,128]{3,2,1,0:T(8,128)S(1)} %get-tuple-element.24), channel_id=1, source_target_pairs={{0,1},{1,2},{2,3},{4,5},{5,6},{6,7},{8,9},{9,10},{10,11},{12,13},{... | collective-permute-start | bytes 1158152 | tf_op jit(solution)/shard_map/ppermute | solution.py:22
  338.2 10.0 %collective-permute-start.7 = (f32[1,58,13,128]{3,2,1,0:T(8,128)S(1)}, f32[1,58,13,128]{3,2,1,0:T(8,128)S(1)}, u32[]{:S(2)}, u32[]{:S(2)}) collective-permute-start(f32[1,58,13,128]{3,2,1,0:T(8,128)S(1)} %get-tuple-element.25), channel_id=1, source_target_pairs={{1,0},{2,1},{3,2},{5,4},{6,5},{7,6},{9,8},{10,9},{11,10},{13,12},{... | collective-permute-start | bytes 1158152 | tf_op jit(solution)/shard_map/ppermute | solution.py:25
  519.0 1.0 copy-start.5
where the time goes:
time: 529 us; the launch traced here: 522 us
  other arithmetic  448 us (85%)
  waiting for transfers between devices  35.6 us (7%)
  starting transfers between devices  22.3 us (4%)
  local copies, waits for them, and re-layouts  14.4 us (3%)
    another operation x14, other arithmetic, apply_plan(): return jnp.stack(results)  260 us
    add x5, other arithmetic, taps_sum(): summed + taps[offset] * lax.slice_in_dim(padded, offset, offset + length,...  139 us
    concatenate x2, other arithmetic, with_halo(): block = jnp.concatenate([low, block, high], axis=dim)  32.4 us
    ppermute x4, waiting for transfers between devices, with_halo(): lax.ppermute(lax.slice_in_dim(block, block.shape[dim] - width, None, axis...  22.8 us
    ppermute x4, starting transfers between devices, with_halo(): lax.ppermute(lax.slice_in_dim(block, block.shape[dim] - width, None, axis...  14.2 us
    ppermute x4, waiting for transfers between devices, with_halo(): lax.ppermute(lax.slice_in_dim(block, 0, width, axis=dim), axis, backward)  12.8 us
  transfers between devices with their start and end apart: 8, of which 7 were waited for; matrix products, arithmetic and copies ran while one was open for 1% of the time, Pallas kernels for 0%

commit v1 on v0

v1 whole, which is shorter than its diff:
```python
import functools

import jax
import jax.numpy as jnp
from jax import lax
from jax.experimental import pallas as pl
from jax.experimental.pallas import tpu as pltpu
from jax.sharding import PartitionSpec as P

UPDATES = 2
TAPS = 25
REACH = TAPS // 2
HALO = REACH + 1
SIDE = 16
F32 = jnp.float32
BF16 = jnp.bfloat16
MESH = pl.DeviceIdType.MESH


def split(value):
    high = value.astype(BF16)
    low = (value - high.astype(F32)).astype(BF16)
    return high, low


def toeplitz(offset, keep, taps):
    out = jnp.zeros(offset.shape, F32)
    for k in range(TAPS):
        out = jnp.where(offset == k, taps[k], out)
    if keep is not None:
        out = jnp.where(keep, out, 0.0)
    return out


def divisor(count, limit):
    return max(d for d in range(1, limit + 1) if count % d == 0)


def kernel(
    nx, ny,
    smooth, slope, band, time_step, phi_hbm, sens_hbm,
    out,
    field, part, grad, mag, vel, speed, zmat, ymat,
    send_sem, recv_sem, local_sem,
):
    rows_x, rows_y, depth = out.shape
    ext_x = rows_x + 2 * HALO
    ext_y = rows_y + 2 * SIDE
    out_y = rows_y + 8
    px = lax.axis_index("gx")
    py = lax.axis_index("gy")
    has = {
        "x-": px > 0, "x+": px < nx - 1, "y-": py > 0, "y+": py < ny - 1,
    }
    peer = {
        "x-": (px - 1, py), "x+": (px + 1, py), "y-": (px, py - 1), "y+": (px, py + 1),
    }
    opposite = {"x-": "x+", "x+": "x-", "y-": "y+", "y+": "y-"}
    own_x = pl.ds(HALO, rows_x)
    own_y = pl.ds(SIDE, rows_y)
    low_x, high_x = pl.ds(0, HALO), pl.ds(HALO + rows_x, HALO)
    low_y, high_y = pl.ds(0, SIDE), pl.ds(SIDE + rows_y, SIDE)

    barrier = pltpu.get_barrier_semaphore()
    for side in has:
        @pl.when(has[side])
        def _(side=side):
            pl.semaphore_signal(barrier, inc=1, device_id=peer[side], device_id_type=MESH)

    local = [
        pltpu.make_async_copy(source, field.at[f, own_x, own_y], local_sem.at[f])
        for f, source in enumerate((phi_hbm, sens_hbm))
    ]
    for copy in local:
        copy.start()

    def source_of(f, xs, ys):
        if f == 2:
            return field.at[f, pl.ds(HALO + xs[0], xs[1]), pl.ds(SIDE + ys[0], ys[1])]
        return (phi_hbm, sens_hbm)[f].at[pl.ds(xs[0], xs[1]), pl.ds(ys[0], ys[1])]

    def remote(f, kind):
        sides = ("x+", "x-", "y+", "y-", "y+", "y+", "y-", "y-")
        side = sides[kind]
        if kind == 0:
            src = source_of(f, (rows_x - HALO, HALO), (0, rows_y))
            dst = field.at[f, low_x, own_y]
        elif kind == 1:
            src = source_of(f, (0, HALO), (0, rows_y))
            dst = field.at[f, high_x, own_y]
        elif kind == 2:
            src = source_of(f, (0, rows_x), (rows_y - SIDE, SIDE))
            dst = field.at[f, own_x, low_y]
        elif kind == 3:
            src = source_of(f, (0, rows_x), (0, SIDE))
            dst = field.at[f, own_x, high_y]
        else:
            xs = low_x if kind in (4, 6) else high_x
            ys = pl.ds(rows_y, SIDE) if side == "y+" else pl.ds(SIDE, SIDE)
            src = field.at[f, xs, ys]
            dst = field.at[f, xs, low_y if side == "y+" else high_y]
        copy = pltpu.make_async_remote_copy(
            src_ref=src, dst_ref=dst,
            send_sem=send_sem.at[f, kind], recv_sem=recv_sem.at[f, kind],
            device_id=peer[side], device_id_type=MESH,
        )
        sends, receives = has[side], has[opposite[side]]
        if kind >= 4:
            there = has["x-"] if kind in (4, 6) else has["x+"]
            sends, receives = sends & there, receives & there
        return copy, sends, receives

    def start(f, kinds):
        for kind in kinds:
            copy, sends, _ = remote(f, kind)
            pl.when(sends)(copy.start)

    def arrived(f, kinds):
        for kind in kinds:
            copy, _, receives = remote(f, kind)
            pl.when(receives)(copy.wait_recv)

    def sent(f, kinds):
        for kind in kinds:
            copy, sends, _ = remote(f, kind)
            pl.when(sends)(copy.wait_send)

    neighbours = sum(has[side].astype(jnp.int32) for side in has)
    pl.semaphore_wait(barrier, neighbours)
    start(0, (0, 1, 2, 3))
    start(1, (0, 1, 2, 3))

    for f in range(3):
        @pl.when(px == 0)
        def _(f=f):
            field[f, low_x] = jnp.zeros((HALO, ext_y, depth), F32)

        @pl.when(px == nx - 1)
        def _(f=f):
            field[f, high_x] = jnp.zeros((HALO, ext_y, depth), F32)

        @pl.when(py == 0)
        def _(f=f):
            field[f, :, low_y] = jnp.zeros((ext_x, SIDE, depth), F32)

        @pl.when(py == ny - 1)
        def _(f=f):
            field[f, :, high_y] = jnp.zeros((ext_x, SIDE, depth), F32)

    offset = (
        lax.broadcasted_iota(jnp.int32, (depth, depth), 0)
        - lax.broadcasted_iota(jnp.int32, (depth, depth), 1) + REACH
    )
    for n, taps in enumerate((smooth, slope)):
        high, low = split(toeplitz(offset, None, taps))
        cols = pl.ds(n * depth, depth)
        zmat[pl.ds(0, depth), cols] = high
        zmat[pl.ds(depth, depth), cols] = high
        zmat[pl.ds(2 * depth, depth), cols] = low
    row = lax.broadcasted_iota(jnp.int32, (out_y, ext_y), 0)
    cell = jnp.where(row == out_y - 1, -1, row)
    keep = (cell <= rows_y) & ((cell >= 0) | (py > 0)) & ((cell < rows_y) | (py < ny - 1))
    offset = lax.broadcasted_iota(jnp.int32, (out_y, ext_y), 1) - cell - (SIDE - REACH)
    pieces = []
    for taps in (smooth, slope):
        high, low = split(toeplitz(offset, keep, taps))
        pieces.append(jnp.concatenate([high.astype(F32), high.astype(F32), low.astype(F32)], axis=1))
    ymat[...] = jnp.concatenate(pieces, axis=0).astype(BF16)

    def planes(f, rows):
        for r in rows:
            high, low = split(field[f, r])
            lhs = jnp.concatenate([high, low, high], axis=1)
            if f == 1:
                z_out = jnp.dot(lhs, zmat[:, :depth], preferred_element_type=F32)
            else:
                z_out = jnp.dot(lhs, zmat[...], preferred_element_type=F32)
            high, low = split(z_out)
            rhs = jnp.concatenate([high, low, high], axis=0)
            if f == 1:
                part[3, r] = jnp.dot(ymat[:out_y], rhs, preferred_element_type=F32)
            else:
                y_out = jnp.dot(ymat[...], rhs, preferred_element_type=F32)
                part[0, r] = y_out[:out_y, :depth]
                part[1, r] = y_out[out_y:, :depth]
                part[2, r] = y_out[:out_y, depth:]

    def own_planes(f):
        step = divisor(rows_x, 8)

        def body(i, carry):
            planes(f, [HALO + i * step + r for r in range(step)])
            return carry

        lax.fori_loop(0, rows_x // step, body, 0)

    def halo_planes(f):
        def body(i, carry):
            planes(f, [i, HALO + rows_x + i])
            return carry

        lax.fori_loop(0, HALO, body, 0)

    group = divisor(rows_x + 2, 17)
    tiles = out_y // 8
    steps = tiles * ((rows_x + 2) // group)

    def smooth_x(n, first, rows):
        acc = [None] * group
        for j in range(group + TAPS - 1):
            value = part[n, first + j, rows]
            for g in range(max(0, j - TAPS + 1), min(group, j + 1)):
                term = smooth[j - g] * value
                acc[g] = term if acc[g] is None else acc[g] + term
        return acc

    def slope_x(n, first, rows):
        values = [part[n, first + j, rows] for j in range(group + TAPS - 1)]
        acc = []
        for g in range(group):
            total = None
            for k in range(REACH):
                term = slope[REACH + 1 + k] * (values[g + REACH + 1 + k] - values[g + REACH - 1 - k])
                total = term if total is None else total + term
            acc.append(total)
        return acc

    def place(i):
        return (i // tiles) * group, pl.ds(pl.multiple_of((i % tiles) * 8, 8), 8)

    def normals():
        def body(i, carry):
            first, rows = place(i)
            for g, value in enumerate(slope_x(0, first, rows)):
                grad[0, first + g, rows] = value
            for g, value in enumerate(smooth_x(1, first, rows)):
                grad[1, first + g, rows] = value
            for g, gz in enumerate(smooth_x(2, first, rows)):
                gx = grad[0, first + g, rows]
                gy = grad[1, first + g, rows]
                square = gx * gx + gy * gy + gz * gz + 1.0
                inverse = lax.rsqrt(square)
                grad[0, first + g, rows] = gx * inverse
                grad[1, first + g, rows] = gy * inverse
                grad[2, first + g, rows] = gz * inverse
                mag[first + g, rows] = square * inverse
            return carry

        lax.fori_loop(0, steps, body, 0)
        for edge, at in ((px == 0, 0), (px == nx - 1, rows_x + 1)):
            @pl.when(edge)
            def _(at=at):
                grad[0, at] = jnp.zeros((out_y, depth), F32)

    def velocity():
        def body(i, carry):
            first, rows = place(i)
            for g, value in enumerate(smooth_x(3, first, rows)):
                vel[first + g, rows] = value
            return carry

        lax.fori_loop(0, steps, body, 0)
        for edge, at in ((px == 0, 0), (px == nx - 1, rows_x + 1)):
            @pl.when(edge)
            def _(at=at):
                vel[at] = jnp.zeros((out_y, depth), F32)

    lane = lax.broadcasted_iota(jnp.int32, (rows_y, depth), 1)

    def around_y(value):
        after = pltpu.roll(value, out_y - 1, 0)[:rows_y]
        before = pltpu.roll(value, 1, 0)[:rows_y]
        return after, before

    def around_z(value):
        after = jnp.where(lane == depth - 1, 0.0, pltpu.roll(value, depth - 1, 1))
        before = jnp.where(lane == 0, 0.0, pltpu.roll(value, 1, 1))
        return after, before

    def speeds():
        def body(x, carry):
            value = vel[x + 1]
            after_y, before_y = around_y(value)
            inner = value[:rows_y]
            after_z, before_z = around_z(inner)
            total = inner + vel[x + 2, :rows_y] + vel[x, :rows_y]
            total = total + after_y + before_y + after_z + before_z
            speed[x] = total * (1.0 / 7.0)
            return carry

        lax.fori_loop(0, rows_x, body, 0)

    blocks_x, blocks_y, blocks_z = band.shape
    wide_x, wide_y, wide_z = rows_x // blocks_x, rows_y // blocks_y, depth // blocks_z
    lane_row = lax.broadcasted_iota(jnp.int32, (wide_y, depth), 1)

    def advance(f, store):
        for p in range(blocks_x):
            strips = []
            for q in range(blocks_y):
                strip = jnp.zeros((wide_y, depth), F32)
                for r in range(blocks_z):
                    entry = band[p, q, r].astype(F32) * time_step[0]
                    strip = jnp.where((lane_row >= r * wide_z) & (lane_row < (r + 1) * wide_z), entry, strip)
                strips.append(strip)
            step_size = jnp.concatenate(strips, axis=0)

            def body(i, carry):
                x = p * wide_x + i
                after_y, before_y = around_y(grad[1, x + 1])
                after_z, before_z = around_z(grad[2, x + 1, :rows_y])
                curvature = 0.5 * (
                    (grad[0, x + 2, :rows_y] - grad[0, x, :rows_y])
                    + (after_y - before_y) + (after_z - before_z)
                )
                phi = field[f, HALO + x, own_y]
                store(x, phi - step_size * mag[x + 1, :rows_y] * (speed[x] - 0.5 * curvature))
                return carry

            lax.fori_loop(0, wide_x, body, 0)

    def store_next(x, value):
        field[2, HALO + x, own_y] = value

    def store_out(x, value):
        out[x] = value

    local[0].wait()
    arrived(0, (2, 3))
    own_planes(0)
    local[1].wait()
    arrived(0, (0, 1))
    start(0, (4, 5, 6, 7))
    arrived(1, (2, 3))
    own_planes(1)
    arrived(0, (4, 5, 6, 7))
    halo_planes(0)
    normals()
    arrived(1, (0, 1))
    start(1, (4, 5, 6, 7))
    arrived(1, (4, 5, 6, 7))
    halo_planes(1)
    velocity()
    speeds()
    advance(0, store_next)
    start(2, (0, 1, 2, 3))
    arrived(2, (2, 3))
    own_planes(2)
    arrived(2, (0, 1))
    start(2, (4, 5, 6, 7))
    arrived(2, (4, 5, 6, 7))
    halo_planes(2)
    normals()
    advance(2, store_out)
    for f in range(3):
        sent(f, range(8))


def per_device(nx, ny, level_set, sensitivity, smooth_taps, slope_taps, band, time_step):
    rows_x, rows_y, depth = level_set.shape
    ext_x = rows_x + 2 * HALO
    ext_y = rows_y + 2 * SIDE
    out_y = rows_y + 8
    smem = pl.BlockSpec(memory_space=pltpu.SMEM)
    hbm = pl.BlockSpec(memory_space=pl.ANY)
    return pl.pallas_call(
        functools.partial(kernel, nx, ny),
        out_shape=jax.ShapeDtypeStruct(level_set.shape, F32),
        in_specs=[smem, smem, smem, smem, hbm, hbm],
        out_specs=pl.BlockSpec(memory_space=pltpu.VMEM),
        scratch_shapes=[
            pltpu.VMEM((3, ext_x, ext_y, depth), F32),
            pltpu.VMEM((4, ext_x, out_y, depth), F32),
            pltpu.VMEM((3, rows_x + 2, out_y, depth), F32),
            pltpu.VMEM((rows_x + 2, out_y, depth), F32),
            pltpu.VMEM((rows_x + 2, out_y, depth), F32),
            pltpu.VMEM((rows_x, rows_y, depth), F32),
            pltpu.VMEM((3 * depth, 2 * depth), BF16),
            pltpu.VMEM((2 * out_y, 3 * ext_y), BF16),
            pltpu.SemaphoreType.DMA((3, 8)),
            pltpu.SemaphoreType.DMA((3, 8)),
            pltpu.SemaphoreType.DMA((2,)),
        ],
        compiler_params=pltpu.CompilerParams(
            collective_id=0, has_side_effects=True, vmem_limit_bytes=40 * 1024 * 1024,
        ),
        name="level_set_updates",
    )(smooth_taps, slope_taps, band, time_step, level_set, sensitivity)


def solution(mesh):
    return jax.shard_map(
        functools.partial(per_device, mesh.shape["gx"], mesh.shape["gy"]),
        mesh=mesh,
        in_specs=(P("gx", "gy", None), P("gx", "gy", None), P(), P(), P("gx", "gy", None), P()),
        out_specs=P("gx", "gy", None),
        check_vma=False,
    )
```

time: 529 us -> 84.2 us (0.16); the launches traced: 522 us -> 83.9 us
  other arithmetic: 448 us -> 0 us
  Pallas kernels: 0 us -> 79.7 us
  waiting for transfers between devices: 35.6 us -> 0 us
  starting transfers between devices: 22.3 us -> 0 us
  local copies, waits for them, and re-layouts: 14.4 us -> 3.56 us
    another operation x14 -> x0, other arithmetic: 260 us -> none  [apply_plan(): return jnp.stack(results)]
    add x5 -> x0, other arithmetic: 139 us -> none  [taps_sum(): summed + taps[offset] * lax.slice_in_dim(padded, offset, offset + length,...]
    pallas_call x0 -> x1, Pallas kernels: none -> 79.7 us  [per_device(): pl.pallas_call(functools.partial(kernel, nx, ny), out_shape=jax.ShapeDtyp...]
    ppermute x8 -> x0, waiting for transfers between devices: 35.6 us -> none  [the longest x4 22.8 us: with_halo(): lax.ppermute(lax.slice_in_dim(block, block.shape[dim] - width, None, axis...]
    concatenate x2 -> x0, other arithmetic: 32.4 us -> none  [with_halo(): block = jnp.concatenate([low, block, high], axis=dim)]
    ppermute x8 -> x0, starting transfers between devices: 22.3 us -> none  [the longest x4 14.2 us: with_halo(): lax.ppermute(lax.slice_in_dim(block, block.shape[dim] - width, None, axis...]
    slice x8 -> x0, local copies, waits for them, and re-layouts: 7.64 us -> none  [the longest x1 4.68 us: apply_plan(): padded[source]]
    slice x2 -> x0, other arithmetic: 7.34 us -> none  [with_halo(): lax.slice_in_dim(block, block.shape[dim] - width, None, axis=dim)]
  transfers between devices with their start and end apart: 8 -> 0, of which waited for: 7 -> 0; matrix products, arithmetic and copies ran while one was open for 1% -> 0% of each run, Pallas kernels for 0% -> 0%
where the time goes in v1:
time: 84.2 us; the launch traced here: 83.9 us
  Pallas kernels  79.7 us (95%)
  local copies, waits for them, and re-layouts  3.56 us (4%)
    pallas_call x1, Pallas kernels, per_device(): pl.pallas_call(functools.partial(kernel, nx, ny), out_shape=jax.ShapeDtyp...  79.7 us
    unnamed x11, local copies, waits for them, and re-layouts  3.56 us

profile of v1, /device:TPU:19, one launch (start us, length us, event | category | flops | bytes accessed | tf_op | source)
XLA Modules:
  0.0 83.9 jit_solution(13746844319166987506)
XLA Ops:
  0.0 0.0 copy-start.4
  0.0 0.0 copy-start.3
  0.7 0.0 copy-done.4
  0.7 0.0 copy-done.3
  0.7 0.0 copy-start
  0.7 1.0 %copy-done = f32[32,32,128]{2,1,0:T(8,128)S(1)} copy-done((f32[32,32,128]{2,1,0:T(8,128)S(1)}, f32[32,32,128]{2,1,0:T(8,128)}, u32[]{:S(2)}) %copy-start) | copy-done | bytes 524312
  1.7 0.0 copy-start.1
  1.7 1.0 %copy-done.1 = f32[32,32,128]{2,1,0:T(8,128)S(1)} copy-done((f32[32,32,128]{2,1,0:T(8,128)S(1)}, f32[32,32,128]{2,1,0:T(8,128)}, u32[]{:S(2)}) %copy-start.1) | copy-done | bytes 524312
  2.8 0.0 copy-start.2
  2.8 0.7 copy-done.2
  3.5 79.7 %level_set_updates.1 = f32[32,32,128]{2,1,0:T(8,128)S(1)} custom-call(f32[25]{0:T(128)S(1)} %copy-done.3, f32[25]{0:T(128)S(1)} %copy-done.4, s32[2,2,4]{2,1,0:T(2,128)S(1)} %copy-done.2, f32[1]{0:T(128)S(6)} %copy.8.time_step, f32[32,32,128]{2,1,0:T(8,128)S(1)} %copy-done, f32[32,32,128]{2,1,0:T(8,128)S(1)} %copy-done.1), custom_call_target="tpu_custom_call" | custom-call | tf_op jit(solution)/shard_map/level_set_updates/pallas_call | solution.py:366
  83.2 0.8 copy.9
Async XLA Ops:
  0.0 0.7 copy-start.4
  0.0 0.7 copy-start.3
  0.7 1.0 %copy-start = (f32[32,32,128]{2,1,0:T(8,128)S(1)}, f32[32,32,128]{2,1,0:T(8,128)}, u32[]{:S(2)}) copy-start(f32[32,32,128]{2,1,0:T(8,128)} %phi_hbm.1) | copy-start | bytes 1572868
  1.7 1.0 %copy-start.1 = (f32[32,32,128]{2,1,0:T(8,128)S(1)}, f32[32,32,128]{2,1,0:T(8,128)}, u32[]{:S(2)}) copy-start(f32[32,32,128]{2,1,0:T(8,128)} %sens_hbm.1) | copy-start | bytes 1572868
  2.8 0.7 copy-start.2

commit v2 on v1

--- a/solution.py
+++ b/solution.py
@@ -167,39 +167,44 @@
         pieces.append(jnp.concatenate([high.astype(F32), high.astype(F32), low.astype(F32)], axis=1))
     ymat[...] = jnp.concatenate(pieces, axis=0).astype(BF16)
 
-    def planes(f, rows):
-        for r in rows:
-            high, low = split(field[f, r])
-            lhs = jnp.concatenate([high, low, high], axis=1)
-            if f == 1:
-                z_out = jnp.dot(lhs, zmat[:, :depth], preferred_element_type=F32)
-            else:
-                z_out = jnp.dot(lhs, zmat[...], preferred_element_type=F32)
-            high, low = split(z_out)
-            rhs = jnp.concatenate([high, low, high], axis=0)
-            if f == 1:
-                part[3, r] = jnp.dot(ymat[:out_y], rhs, preferred_element_type=F32)
-            else:
-                y_out = jnp.dot(ymat[...], rhs, preferred_element_type=F32)
-                part[0, r] = y_out[:out_y, :depth]
-                part[1, r] = y_out[out_y:, :depth]
-                part[2, r] = y_out[:out_y, depth:]
+    def planes(f, first, count):
+        high, low = split(field[f, pl.ds(first, count)].reshape(count * ext_y, depth))
+        lhs = jnp.concatenate([high, low, high], axis=1)
+        width = depth if f == 1 else 2 * depth
+        high, low = split(jnp.dot(lhs, zmat[:, :width], preferred_element_type=F32))
+
+        def stack(r):
+            rows = slice(r * ext_y, (r + 1) * ext_y)
+            return jnp.concatenate([high[rows], low[rows], high[rows]], axis=0)
+
+        if f == 1:
+            for r in range(0, count, 2):
+                both = [stack(q) for q in range(r, min(r + 2, count))]
+                y_out = jnp.dot(ymat[:out_y], jnp.concatenate(both, axis=1), preferred_element_type=F32)
+                for q in range(len(both)):
+                    part[3, first + r + q] = y_out[:, q * depth:(q + 1) * depth]
+        else:
+            for r in range(count):
+                y_out = jnp.dot(ymat[...], stack(r), preferred_element_type=F32)
+                part[0, first + r] = y_out[:out_y, :depth]
+                part[1, first + r] = y_out[out_y:, :depth]
+                part[2, first + r] = y_out[:out_y, depth:]
 
     def own_planes(f):
-        step = divisor(rows_x, 8)
+        step = divisor(rows_x, 16)
 
         def body(i, carry):
-            planes(f, [HALO + i * step + r for r in range(step)])
+            planes(f, HALO + i * step, step)
             return carry
 
         lax.fori_loop(0, rows_x // step, body, 0)
 
     def halo_planes(f):
         def body(i, carry):
-            planes(f, [i, HALO + rows_x + i])
+            planes(f, i * (HALO + rows_x), HALO)
             return carry
 
-        lax.fori_loop(0, HALO, body, 0)
+        lax.fori_loop(0, 2, body, 0)
 
     group = divisor(rows_x + 2, 17)
     tiles = out_y // 8
@@ -278,17 +283,21 @@
         return after, before
 
     def speeds():
-        def body(x, carry):
-            value = vel[x + 1]
-            after_y, before_y = around_y(value)
-            inner = value[:rows_y]
-            after_z, before_z = around_z(inner)
-            total = inner + vel[x + 2, :rows_y] + vel[x, :rows_y]
-            total = total + after_y + before_y + after_z + before_z
-            speed[x] = total * (1.0 / 7.0)
+        step = divisor(rows_x, 4)
+
+        def body(i, carry):
+            for u in range(step):
+                x = i * step + u
+                value = vel[x + 1]
+                after_y, before_y = around_y(value)
+                inner = value[:rows_y]
+                after_z, before_z = around_z(inner)
+                total = inner + vel[x + 2, :rows_y] + vel[x, :rows_y]
+                total = total + after_y + before_y + after_z + before_z
+                speed[x] = total * (1.0 / 7.0)
             return carry
 
-        lax.fori_loop(0, rows_x, body, 0)
+        lax.fori_loop(0, rows_x // step, body, 0)
 
     blocks_x, blocks_y, blocks_z = band.shape
     wide_x, wide_y, wide_z = rows_x // blocks_x, rows_y // blocks_y, depth // blocks_z
@@ -305,19 +314,22 @@
                 strips.append(strip)
             step_size = jnp.concatenate(strips, axis=0)
 
+            step = divisor(wide_x, 4)
+
             def body(i, carry):
-                x = p * wide_x + i
-                after_y, before_y = around_y(grad[1, x + 1])
-                after_z, before_z = around_z(grad[2, x + 1, :rows_y])
-                curvature = 0.5 * (
-                    (grad[0, x + 2, :rows_y] - grad[0, x, :rows_y])
-                    + (after_y - before_y) + (after_z - before_z)
-                )
-                phi = field[f, HALO + x, own_y]
-                store(x, phi - step_size * mag[x + 1, :rows_y] * (speed[x] - 0.5 * curvature))
+                for u in range(step):
+                    x = p * wide_x + i * step + u
+                    after_y, before_y = around_y(grad[1, x + 1])
+                    after_z, before_z = around_z(grad[2, x + 1, :rows_y])
+                    curvature = 0.5 * (
+                        (grad[0, x + 2, :rows_y] - grad[0, x, :rows_y])
+                        + (after_y - before_y) + (after_z - before_z)
+                    )
+                    phi = field[f, HALO + x, own_y]
+                    store(x, phi - step_size * mag[x + 1, :rows_y] * (speed[x] - 0.5 * curvature))
                 return carry
 
-            lax.fori_loop(0, wide_x, body, 0)
+            lax.fori_loop(0, wide_x // step, body, 0)
 
     def store_next(x, value):
         field[2, HALO + x, own_y] = value

time: 84.2 us -> 60.1 us (0.71)
  Pallas kernels: 79.7 us -> 55.1 us
    pallas_call x1, Pallas kernels: 79.7 us -> 55.1 us  [per_device(): pl.pallas_call(functools.partial(kernel, nx, ny), out_shape=jax.ShapeDtyp...]
where the time goes in v2:
time: 60.1 us; the launch traced here: 59.3 us
  Pallas kernels  55.1 us (92%)
  local copies, waits for them, and re-layouts  3.56 us (6%)
  between operations  0.72 us (1%)
    pallas_call x1, Pallas kernels, per_device(): pl.pallas_call(functools.partial(kernel, nx, ny), out_shape=jax.ShapeDtyp...  55.1 us
    unnamed x11, local copies, waits for them, and re-layouts  3.56 us

profile of v2, /device:TPU:19, one launch (start us, length us, event | category | flops | bytes accessed | tf_op | source)
XLA Modules:
  0.0 59.3 jit_solution(4017506979085136928)
XLA Ops:
  0.0 0.0 copy-start.4
  0.0 0.0 copy-start.3
  0.7 0.0 copy-done.4
  0.7 0.0 copy-done.3
  0.7 0.0 copy-start
  0.7 1.0 %copy-done = f32[32,32,128]{2,1,0:T(8,128)S(1)} copy-done((f32[32,32,128]{2,1,0:T(8,128)S(1)}, f32[32,32,128]{2,1,0:T(8,128)}, u32[]{:S(2)}) %copy-start) | copy-done | bytes 524312
  1.7 0.0 copy-start.1
  1.7 1.0 %copy-done.1 = f32[32,32,128]{2,1,0:T(8,128)S(1)} copy-done((f32[32,32,128]{2,1,0:T(8,128)S(1)}, f32[32,32,128]{2,1,0:T(8,128)}, u32[]{:S(2)}) %copy-start.1) | copy-done | bytes 524312
  2.8 0.0 copy-start.2
  2.8 0.7 %copy-done.2 = s32[2,2,4]{2,1,0:T(2,128)S(1)} copy-done((s32[2,2,4]{2,1,0:T(2,128)S(1)}, s32[2,2,4]{2,1,0:T(2,128)}, u32[]{:S(2)}) %copy-start.2) | copy-done | bytes 88
  3.5 55.1 %level_set_updates.1 = f32[32,32,128]{2,1,0:T(8,128)S(1)} custom-call(f32[25]{0:T(128)S(1)} %copy-done.3, f32[25]{0:T(128)S(1)} %copy-done.4, s32[2,2,4]{2,1,0:T(2,128)S(1)} %copy-done.2, f32[1]{0:T(128)S(6)} %copy.8.time_step, f32[32,32,128]{2,1,0:T(8,128)S(1)} %copy-done, f32[32,32,128]{2,1,0:T(8,128)S(1)} %copy-done.1), custom_call_target="tpu_custom_call" | custom-call | tf_op jit(solution)/shard_map/level_set_updates/pallas_call | solution.py:378
  58.6 0.8 %copy.9 = f32[32,32,128]{2,1,0:T(8,128)} copy(f32[32,32,128]{2,1,0:T(8,128)S(1)} %level_set_updates.1) | data formatting | bytes 1048576
Async XLA Ops:
  0.0 0.7 %copy-start.4 = (f32[25]{0:T(128)S(1)}, f32[25]{0:T(128)}, u32[]{:S(2)}) copy-start(f32[25]{0:T(128)} %slope.1) | copy-start | bytes 304
  0.0 0.7 %copy-start.3 = (f32[25]{0:T(128)S(1)}, f32[25]{0:T(128)}, u32[]{:S(2)}) copy-start(f32[25]{0:T(128)} %smooth.1) | copy-start | bytes 304
  0.7 1.0 %copy-start = (f32[32,32,128]{2,1,0:T(8,128)S(1)}, f32[32,32,128]{2,1,0:T(8,128)}, u32[]{:S(2)}) copy-start(f32[32,32,128]{2,1,0:T(8,128)} %phi_hbm.1) | copy-start | bytes 1572868
  1.7 1.0 %copy-start.1 = (f32[32,32,128]{2,1,0:T(8,128)S(1)}, f32[32,32,128]{2,1,0:T(8,128)}, u32[]{:S(2)}) copy-start(f32[32,32,128]{2,1,0:T(8,128)} %sens_hbm.1) | copy-start | bytes 1572868
  2.8 0.7 %copy-start.2 = (s32[2,2,4]{2,1,0:T(2,128)S(1)}, s32[2,2,4]{2,1,0:T(2,128)}, u32[]{:S(2)}) copy-start(s32[2,2,4]{2,1,0:T(2,128)} %band.1) | copy-start | bytes 196

commit v3 on v2

--- a/solution.py
+++ b/solution.py
@@ -79,35 +79,42 @@
             return field.at[f, pl.ds(HALO + xs[0], xs[1]), pl.ds(SIDE + ys[0], ys[1])]
         return (phi_hbm, sens_hbm)[f].at[pl.ds(xs[0], xs[1]), pl.ds(ys[0], ys[1])]
 
+    cut = HALO - HALO // 2
+    pieces = ((0, cut), (cut, HALO - cut))
+    first_x = {"x-": 0, "x+": HALO + rows_x}
+    mains = (0, 1)
+    edges = tuple((2 + 6 * n, 3 + 6 * n) for n in range(2))
+    corners = tuple(tuple(range(4 + 6 * n, 8 + 6 * n)) for n in range(2))
+
     def remote(f, kind):
-        sides = ("x+", "x-", "y+", "y-", "y+", "y+", "y-", "y-")
-        side = sides[kind]
-        if kind == 0:
-            src = source_of(f, (rows_x - HALO, HALO), (0, rows_y))
-            dst = field.at[f, low_x, own_y]
-        elif kind == 1:
-            src = source_of(f, (0, HALO), (0, rows_y))
-            dst = field.at[f, high_x, own_y]
-        elif kind == 2:
-            src = source_of(f, (0, rows_x), (rows_y - SIDE, SIDE))
-            dst = field.at[f, own_x, low_y]
-        elif kind == 3:
-            src = source_of(f, (0, rows_x), (0, SIDE))
-            dst = field.at[f, own_x, high_y]
+        there = None
+        if kind in mains:
+            side = ("y+", "y-")[kind]
+            ys = (rows_y - SIDE, SIDE) if side == "y+" else (0, SIDE)
+            src = source_of(f, (0, rows_x), ys)
+            dst = field.at[f, own_x, low_y if side == "y+" else high_y]
         else:
-            xs = low_x if kind in (4, 6) else high_x
-            ys = pl.ds(rows_y, SIDE) if side == "y+" else pl.ds(SIDE, SIDE)
-            src = field.at[f, xs, ys]
-            dst = field.at[f, xs, low_y if side == "y+" else high_y]
+            at, size = pieces[(kind - 2) // 6]
+            which = (kind - 2) % 6
+            if which < 2:
+                side = ("x+", "x-")[which]
+                begin = rows_x - HALO + at if side == "x+" else at
+                src = source_of(f, (begin, size), (0, rows_y))
+                dst = field.at[f, pl.ds(first_x[opposite[side]] + at, size), own_y]
+            else:
+                side = ("y+", "y-")[(which - 2) // 2]
+                there = ("x-", "x+")[(which - 2) % 2]
+                xs = pl.ds(first_x[there] + at, size)
+                src = field.at[f, xs, pl.ds(rows_y if side == "y+" else SIDE, SIDE)]
+                dst = field.at[f, xs, low_y if side == "y+" else high_y]
         copy = pltpu.make_async_remote_copy(
             src_ref=src, dst_ref=dst,
             send_sem=send_sem.at[f, kind], recv_sem=recv_sem.at[f, kind],
             device_id=peer[side], device_id_type=MESH,
         )
         sends, receives = has[side], has[opposite[side]]
-        if kind >= 4:
-            there = has["x-"] if kind in (4, 6) else has["x+"]
-            sends, receives = sends & there, receives & there
+        if there is not None:
+            sends, receives = sends & has[there], receives & has[there]
         return copy, sends, receives
 
     def start(f, kinds):
@@ -127,8 +134,8 @@
 
     neighbours = sum(has[side].astype(jnp.int32) for side in has)
     pl.semaphore_wait(barrier, neighbours)
-    start(0, (0, 1, 2, 3))
-    start(1, (0, 1, 2, 3))
+    for f in range(2):
+        start(f, edges[0] + mains + edges[1])
 
     for f in range(3):
         @pl.when(px == 0)
@@ -161,11 +168,11 @@
     cell = jnp.where(row == out_y - 1, -1, row)
     keep = (cell <= rows_y) & ((cell >= 0) | (py > 0)) & ((cell < rows_y) | (py < ny - 1))
     offset = lax.broadcasted_iota(jnp.int32, (out_y, ext_y), 1) - cell - (SIDE - REACH)
-    pieces = []
+    strips = []
     for taps in (smooth, slope):
         high, low = split(toeplitz(offset, keep, taps))
-        pieces.append(jnp.concatenate([high.astype(F32), high.astype(F32), low.astype(F32)], axis=1))
-    ymat[...] = jnp.concatenate(pieces, axis=0).astype(BF16)
+        strips.append(jnp.concatenate([high.astype(F32), high.astype(F32), low.astype(F32)], axis=1))
+    ymat[...] = jnp.concatenate(strips, axis=0).astype(BF16)
 
     def planes(f, first, count):
         high, low = split(field[f, pl.ds(first, count)].reshape(count * ext_y, depth))
@@ -199,72 +206,121 @@
 
         lax.fori_loop(0, rows_x // step, body, 0)
 
-    def halo_planes(f):
+    def halo_planes(f, n):
+        at, size = pieces[n]
+
         def body(i, carry):
-            planes(f, i * (HALO + rows_x), HALO)
+            planes(f, i * (HALO + rows_x) + at, size)
             return carry
 
         lax.fori_loop(0, 2, body, 0)
 
     group = divisor(rows_x + 2, 17)
     tiles = out_y // 8
-    steps = tiles * ((rows_x + 2) // group)
-
-    def smooth_x(n, first, rows):
+
+    def is_own(row):
+        return HALO <= row < HALO + rows_x
+
+    def smooth_x(n, first, rows, own, target):
         acc = [None] * group
         for j in range(group + TAPS - 1):
+            if is_own(first + j) != own:
+                continue
             value = part[n, first + j, rows]
             for g in range(max(0, j - TAPS + 1), min(group, j + 1)):
                 term = smooth[j - g] * value
                 acc[g] = term if acc[g] is None else acc[g] + term
+        return finish(acc, first, rows, own, target)
+
+    def finish(acc, first, rows, own, target):
+        if own:
+            for g in range(group):
+                target(first + g, rows, acc[g])
+            return None
         return acc
 
-    def slope_x(n, first, rows):
-        values = [part[n, first + j, rows] for j in range(group + TAPS - 1)]
+    def slope_x(n, first, rows, own, target):
+        values = {
+            j: part[n, first + j, rows]
+            for j in range(group + TAPS - 1) if is_own(first + j) == own
+        }
         acc = []
         for g in range(group):
             total = None
-            for k in range(REACH):
-                term = slope[REACH + 1 + k] * (values[g + REACH + 1 + k] - values[g + REACH - 1 - k])
+            for k in range(REACH + 1, TAPS):
+                after, before = values.get(g + k), values.get(g + TAPS - 1 - k)
+                if after is None and before is None:
+                    continue
+                if before is None:
+                    pair = after
+                elif after is None:
+                    pair = -before
+                else:
+                    pair = after - before
+                term = slope[k] * pair
                 total = term if total is None else total + term
             acc.append(total)
-        return acc
-
-    def place(i):
-        return (i // tiles) * group, pl.ds(pl.multiple_of((i % tiles) * 8, 8), 8)
+        return finish(acc, first, rows, own, target)
+
+    def each_tile(work):
+        for first in range(0, rows_x + 2, group):
+            def body(i, carry, first=first):
+                work(first, pl.ds(pl.multiple_of(i * 8, 8), 8))
+                return carry
+
+            lax.fori_loop(0, tiles, body, 0)
+
+    def plus(ref_value, extra):
+        return ref_value if extra is None else ref_value + extra
+
+    def put_grad(n):
+        def target(x, rows, value):
+            grad[n, x, rows] = jnp.zeros((8, depth), F32) if value is None else value
+        return target
+
+    def put_vel(x, rows, value):
+        vel[x, rows] = jnp.zeros((8, depth), F32) if value is None else value
+
+    def own_gradients():
+        def work(first, rows):
+            slope_x(0, first, rows, True, put_grad(0))
+            smooth_x(1, first, rows, True, put_grad(1))
+            smooth_x(2, first, rows, True, put_grad(2))
+
+        each_tile(work)
 
     def normals():
-        def body(i, carry):
-            first, rows = place(i)
-            for g, value in enumerate(slope_x(0, first, rows)):
-                grad[0, first + g, rows] = value
-            for g, value in enumerate(smooth_x(1, first, rows)):
-                grad[1, first + g, rows] = value
-            for g, gz in enumerate(smooth_x(2, first, rows)):
-                gx = grad[0, first + g, rows]
-                gy = grad[1, first + g, rows]
+        def work(first, rows):
+            more_x = slope_x(0, first, rows, False, None)
+            more_y = smooth_x(1, first, rows, False, None)
+            more_z = smooth_x(2, first, rows, False, None)
+            for g in range(group):
+                gx = plus(grad[0, first + g, rows], more_x[g])
+                gy = plus(grad[1, first + g, rows], more_y[g])
+                gz = plus(grad[2, first + g, rows], more_z[g])
                 square = gx * gx + gy * gy + gz * gz + 1.0
                 inverse = lax.rsqrt(square)
                 grad[0, first + g, rows] = gx * inverse
                 grad[1, first + g, rows] = gy * inverse
                 grad[2, first + g, rows] = gz * inverse
                 mag[first + g, rows] = square * inverse
-            return carry
-
-        lax.fori_loop(0, steps, body, 0)
+
+        each_tile(work)
         for edge, at in ((px == 0, 0), (px == nx - 1, rows_x + 1)):
             @pl.when(edge)
             def _(at=at):
                 grad[0, at] = jnp.zeros((out_y, depth), F32)
 
+    def own_velocity():
+        each_tile(lambda first, rows: smooth_x(3, first, rows, True, put_vel))
+
     def velocity():
-        def body(i, carry):
-            first, rows = place(i)
-            for g, value in enumerate(smooth_x(3, first, rows)):
-                vel[first + g, rows] = value
-            return carry
-
-        lax.fori_loop(0, steps, body, 0)
+        def work(first, rows):
+            for g, extra in enumerate(smooth_x(3, first, rows, False, None)):
+                if extra is not None:
+                    vel[first + g, rows] = vel[first + g, rows] + extra
+
+        each_tile(work)
         for edge, at in ((px == 0, 0), (px == nx - 1, rows_x + 1)):
             @pl.when(edge)
             def _(at=at):
@@ -338,34 +394,45 @@
         out[x] = value
 
     local[0].wait()
-    arrived(0, (2, 3))
+    arrived(0, mains)
     own_planes(0)
     local[1].wait()
-    arrived(0, (0, 1))
-    start(0, (4, 5, 6, 7))
-    arrived(1, (2, 3))
+    arrived(0, edges[0])
+    start(0, corners[0])
+    own_gradients()
+    arrived(0, edges[1])
+    start(0, corners[1])
+    arrived(1, mains)
     own_planes(1)
-    arrived(0, (4, 5, 6, 7))
-    halo_planes(0)
+    own_velocity()
+    arrived(0, corners[0])
+    halo_planes(0, 0)
+    arrived(0, corners[1])
+    halo_planes(0, 1)
     normals()
-    arrived(1, (0, 1))
-    start(1, (4, 5, 6, 7))
-    arrived(1, (4, 5, 6, 7))
-    halo_planes(1)
+    for n in range(2):
+        arrived(1, edges[n])
+        start(1, corners[n])
+    for n in range(2):
+        arrived(1, corners[n])
+        halo_planes(1, n)
     velocity()
     speeds()
     advance(0, store_next)
-    start(2, (0, 1, 2, 3))
-    arrived(2, (2, 3))
+    start(2, edges[0] + mains + edges[1])
+    arrived(2, mains)
     own_planes(2)
-    arrived(2, (0, 1))
-    start(2, (4, 5, 6, 7))
-    arrived(2, (4, 5, 6, 7))
-    halo_planes(2)
+    own_gradients()
+    for n in range(2):
+        arrived(2, edges[n])
+        start(2, corners[n])
+    for n in range(2):
+        arrived(2, corners[n])
+        halo_planes(2, n)
     normals()
     advance(2, store_out)
     for f in range(3):
-        sent(f, range(8))
+        sent(f, mains + edges[0] + edges[1] + corners[0] + corners[1])
 
 
 def per_device(nx, ny, level_set, sensitivity, smooth_taps, slope_taps, band, time_step):
@@ -389,12 +456,12 @@
             pltpu.VMEM((rows_x, rows_y, depth), F32),
             pltpu.VMEM((3 * depth, 2 * depth), BF16),
             pltpu.VMEM((2 * out_y, 3 * ext_y), BF16),
-            pltpu.SemaphoreType.DMA((3, 8)),
-            pltpu.SemaphoreType.DMA((3, 8)),
+            pltpu.SemaphoreType.DMA((3, 14)),
+            pltpu.SemaphoreType.DMA((3, 14)),
             pltpu.SemaphoreType.DMA((2,)),
         ],
         compiler_params=pltpu.CompilerParams(
-            collective_id=0, has_side_effects=True, vmem_limit_bytes=40 * 1024 * 1024,
+            collective_id=0, has_side_effects=True,
         ),
         name="level_set_updates",
     )(smooth_taps, slope_taps, band, time_step, level_set, sensitivity)

time: 60.1 us -> 54.4 us (0.905)
  Pallas kernels: 55.1 us -> 51.6 us
  local copies, waits for them, and re-layouts: 3.56 us -> 1.87 us
    pallas_call x1, Pallas kernels: 55.1 us -> 51.6 us  [per_device(): pl.pallas_call(functools.partial(kernel, nx, ny), out_shape=jax.ShapeDtyp...]
    unnamed x11 -> x1, local copies, waits for them, and re-layouts: 3.56 us -> 1.87 us
where the time goes in v3:
time: 54.4 us; the launch traced here: 54.1 us
  Pallas kernels  51.6 us (95%)
  local copies, waits for them, and re-layouts  1.87 us (3%)
  between operations  0.66 us (1%)
    pallas_call x1, Pallas kernels, per_device(): pl.pallas_call(functools.partial(kernel, nx, ny), out_shape=jax.ShapeDtyp...  51.6 us
    unnamed x1, local copies, waits for them, and re-layouts  1.87 us

profile of v3, /device:TPU:19, one launch (start us, length us, event | category | flops | bytes accessed | tf_op | source)
XLA Modules:
  0.0 54.1 jit_solution(11111504680618727732)
XLA Ops:
  0.7 51.6 %level_set_updates.1 = f32[32,32,128]{2,1,0:T(8,128)} custom-call(f32[25]{0:T(128)} %smooth.1, f32[25]{0:T(128)} %slope.1, s32[2,2,4]{2,1,0:T(2,128)} %band.1, f32[1]{0:T(128)S(6)} %copy.8.time_step, f32[32,32,128]{2,1,0:T(8,128)} %phi_hbm.1, f32[32,32,128]{2,1,0:T(8,128)} %sens_hbm.1), custom_call_target="tpu_custom_call" | custom-call | tf_op jit(solution)/shard_map/level_set_updates/pallas_call | solution.py:445
  52.2 1.9 %copy.9 = f32[32,32,128]{2,1,0:T(8,128)} copy(f32[32,32,128]{2,1,0:T(8,128)} %level_set_updates.1) | data formatting | bytes 1048576

commit v4 on v3

--- a/solution.py
+++ b/solution.py
@@ -338,28 +338,22 @@
         before = jnp.where(lane == 0, 0.0, pltpu.roll(value, 1, 1))
         return after, before
 
-    def speeds():
-        step = divisor(rows_x, 4)
-
-        def body(i, carry):
-            for u in range(step):
-                x = i * step + u
-                value = vel[x + 1]
-                after_y, before_y = around_y(value)
-                inner = value[:rows_y]
-                after_z, before_z = around_z(inner)
-                total = inner + vel[x + 2, :rows_y] + vel[x, :rows_y]
-                total = total + after_y + before_y + after_z + before_z
-                speed[x] = total * (1.0 / 7.0)
-            return carry
-
-        lax.fori_loop(0, rows_x // step, body, 0)
+    def speed_at(x):
+        value = vel[x + 1]
+        after_y, before_y = around_y(value)
+        inner = value[:rows_y]
+        after_z, before_z = around_z(inner)
+        total = inner + vel[x + 2, :rows_y] + vel[x, :rows_y]
+        total = total + after_y + before_y + after_z + before_z
+        total = total * (1.0 / 7.0)
+        speed[x] = total
+        return total
 
     blocks_x, blocks_y, blocks_z = band.shape
     wide_x, wide_y, wide_z = rows_x // blocks_x, rows_y // blocks_y, depth // blocks_z
     lane_row = lax.broadcasted_iota(jnp.int32, (wide_y, depth), 1)
 
-    def advance(f, store):
+    def advance(f, speed_of, store, after):
         for p in range(blocks_x):
             strips = []
             for q in range(blocks_y):
@@ -382,10 +376,11 @@
                         + (after_y - before_y) + (after_z - before_z)
                     )
                     phi = field[f, HALO + x, own_y]
-                    store(x, phi - step_size * mag[x + 1, :rows_y] * (speed[x] - 0.5 * curvature))
+                    store(x, phi - step_size * mag[x + 1, :rows_y] * (speed_of(x) - 0.5 * curvature))
                 return carry
 
             lax.fori_loop(0, wide_x // step, body, 0)
+            after(p)
 
     def store_next(x, value):
         field[2, HALO + x, own_y] = value
@@ -417,9 +412,16 @@
         arrived(1, corners[n])
         halo_planes(1, n)
     velocity()
-    speeds()
-    advance(0, store_next)
-    start(2, edges[0] + mains + edges[1])
+
+    low_done = -(-HALO // wide_x) - 1
+
+    def send_next(p):
+        if p == low_done:
+            start(2, (edges[0][1], edges[1][1]))
+        if p == blocks_x - 1:
+            start(2, (edges[0][0],) + mains + (edges[1][0],))
+
+    advance(0, speed_at, store_next, send_next)
     arrived(2, mains)
     own_planes(2)
     own_gradients()
@@ -430,7 +432,7 @@
         arrived(2, corners[n])
         halo_planes(2, n)
     normals()
-    advance(2, store_out)
+    advance(2, lambda x: speed[x], store_out, lambda p: None)
     for f in range(3):
         sent(f, mains + edges[0] + edges[1] + corners[0] + corners[1])
 

time: 54.4 us -> 53.8 us (0.989)
  Pallas kernels: 51.6 us -> 51 us
where the time goes in v4:
time: 53.8 us; the launch traced here: 53.6 us
  Pallas kernels  51 us (95%)
  local copies, waits for them, and re-layouts  1.87 us (3%)
  between operations  0.66 us (1%)
    pallas_call x1, Pallas kernels, per_device(): pl.pallas_call(functools.partial(kernel, nx, ny), out_shape=jax.ShapeDtyp...  51 us
    unnamed x1, local copies, waits for them, and re-layouts  1.87 us

profile of v4, /device:TPU:19, one launch (start us, length us, event | category | flops | bytes accessed | tf_op | source)
XLA Modules:
  0.0 53.6 jit_solution(12519695600730673772)
XLA Ops:
  0.7 51.0 %level_set_updates.1 = f32[32,32,128]{2,1,0:T(8,128)} custom-call(f32[25]{0:T(128)} %smooth.1, f32[25]{0:T(128)} %slope.1, s32[2,2,4]{2,1,0:T(2,128)} %band.1, f32[1]{0:T(128)S(6)} %copy.8.time_step, f32[32,32,128]{2,1,0:T(8,128)} %phi_hbm.1, f32[32,32,128]{2,1,0:T(8,128)} %sens_hbm.1), custom_call_target="tpu_custom_call" | custom-call | tf_op jit(solution)/shard_map/level_set_updates/pallas_call | solution.py:447
  51.7 1.9 %copy.9 = f32[32,32,128]{2,1,0:T(8,128)} copy(f32[32,32,128]{2,1,0:T(8,128)} %level_set_updates.1) | data formatting | bytes 1048576
